TPU v7x, 128 devices: a whole 4x4x4 slice. The times are simulated.
128 devices in a mesh: head: 4 (over z_lo, core), track: 32 (over y, z_hi, x).
Axes of the slice: x: 4, y: 4, z: 4 (z_hi: 2, z_lo: 2; z = z_hi * 2 + z_lo), core: 2. Of those that a mesh axis runs over, the one named last changes fastest.
Arguments:
- potential: float32 [256, 4096, 128], P('head', 'track'), may hold values from -6 to 6
- source: float32 [256, 4096, 128], P('head', 'track'), may hold values from -6 to 6
- depth_kernel: float32 [3, 128], replicated, may hold values from -0.5 to 0.5
- magnet: float32 [3, 32, 16384], P(None, 'track', 'head'), may hold values from -0.8 to 0.8
- footprint: int32 [32, 16384], P('track', 'head'), may hold values from 0 to 262143, as said below
- temp_index: int32 [32, 16384], P('track', 'head'), may hold values from 0 to 127
- temp_profile: float32 [128], replicated, may hold values from 0.3 to 1.4
- self_tiles: float32 [32, 128, 128, 128], P('track', 'head'), may hold values from -0.5 to 0.5
- next_tiles: float32 [32, 128, 128, 128], P('track', 'head'), may hold values from -0.5 to 0.5
Outputs:
- relaxed: float32 [256, 4096, 128], P('head', 'track')
- magnet_out: float32 [3, 32, 16384], P(None, 'track', 'head')
Inputs may be any that keep to these rules, and one draw needn't show every extreme that they name: Within the 4096 grains of one device (an aligned block of a track tile), no more than 256 have footprint cells in any one pole block of 8192 cells; in every draw one pole block, the same for every device, takes exactly 256 grains of every device.
All inputs are finite; a program needn't handle non-finite values.
Results may differ from a plain program's by a relative error of at most 0.0001.
Values sent between devices are 32-bit elements; how exact they have to be, the bound alone decides.
A program may use at most 320 MiB of HBM per device.

v0:
```python
import jax
import jax.numpy as jnp
from jax import lax
from jax.sharding import PartitionSpec as P

HIGH = lax.Precision.HIGHEST


def extended(block, sides, width):
    for axis, dim in sides:
        count = lax.axis_size(axis)
        forward = [(i, i + 1) for i in range(count - 1)]
        backward = [(target, source) for source, target in forward]
        low = lax.ppermute(
            lax.slice_in_dim(block, block.shape[dim] - width, None, axis=dim), axis, forward
        )
        high = lax.ppermute(lax.slice_in_dim(block, 0, width, axis=dim), axis, backward)
        block = jnp.concatenate([low, block, high], axis=dim)
    return block


def relax_sweep(padded, source):
    center = padded[1:-1, 1:-1]
    deep = jnp.pad(center, ((0, 0), (0, 0), (1, 1)))
    others = [
        padded[2:, 1:-1],
        padded[:-2, 1:-1],
        padded[1:-1, 2:],
        padded[1:-1, :-2],
        deep[:, :, 2:],
        deep[:, :, :-2],
    ]
    numer = source
    denom = jnp.ones_like(center)
    for other in others:
        differ = other - center
        perm = 1.0 + 4.0 / (1.0 + 4.0 * differ * differ)
        numer = numer + perm * differ
        denom = denom + perm
    return center + 0.8 * numer / denom


def cross_comp(a_vec, b_vec):
    return jnp.stack(
        [
            a_vec[1] * b_vec[2] - a_vec[2] * b_vec[1],
            a_vec[2] * b_vec[0] - a_vec[0] * b_vec[2],
            a_vec[0] * b_vec[1] - a_vec[1] * b_vec[0],
        ]
    )


def llb_section(state, field, target):
    sq_norm = jnp.sum(state * state, axis=0)
    total = field + 0.5 * (1.0 - sq_norm / target) * state
    turn = cross_comp(state, total)
    damp = cross_comp(state, turn)
    along = jnp.sum(state * total, axis=0)
    return state + 0.1 * (-turn - 0.5 * damp + 0.3 * along * state)


def per_device(
    potential,
    source,
    depth_kernel,
    magnet,
    footprint,
    temp_index,
    temp_profile,
    self_tiles,
    next_tiles,
):
    rows_x, rows_y, depth = potential.shape
    relaxed = potential
    for sweep_idx in range(2):
        padded = extended(relaxed, (("head", 0), ("track", 1)), 1)
        relaxed = relax_sweep(padded, source)
    surface = jnp.einsum("kz,xyz->kxy", depth_kernel, relaxed, precision=HIGH).reshape(
        3, rows_x * rows_y
    )
    cells = footprint[0]
    table = lax.all_gather(surface, "track", axis=1, tiled=True)
    applied = jnp.take(table, cells, axis=1)
    n_prof = temp_profile.shape[0]
    onehot = (temp_index[0][None, :] == jnp.arange(n_prof, dtype=jnp.int32)[:, None]).astype(
        jnp.float32
    )
    temp = jnp.dot(temp_profile[None, :], onehot, precision=HIGH)[0]
    target = 0.05 + jnp.maximum(1.0 - temp, 0.0)
    couple_self = self_tiles[0]
    couple_next = next_tiles[0]
    n_tiles, tile_w = (couple_self.shape[0], couple_self.shape[1])
    state = magnet[:, 0, :]
    for section in range(2):
        rimmed = extended(state, (("head", 1),), tile_w)
        tiles = rimmed.reshape(3, n_tiles + 2, tile_w)
        ex = jnp.einsum("kij,ckj->cki", couple_self, tiles[:, 1:-1], precision=HIGH)
        ex = ex + jnp.einsum("kij,ckj->cki", couple_next, tiles[:, :-2], precision=HIGH)
        ex = ex + jnp.einsum("kji,ckj->cki", couple_next, tiles[:, 2:], precision=HIGH)
        state = llb_section(state, applied + ex.reshape(3, n_tiles * tile_w), target)
    return (relaxed, state[:, None, :])


def solution(mesh):
    in_specs = (
        P("head", "track", None),
        P("head", "track", None),
        P(),
        P(None, "track", "head"),
        P("track", "head"),
        P("track", "head"),
        P(),
        P("track", "head", None, None),
        P("track", "head", None, None),
    )
    out_specs = (P("head", "track", None), P(None, "track", "head"))
    return jax.shard_map(
        per_device, mesh=mesh, in_specs=in_specs, out_specs=out_specs, check_vma=False
    )
```

profile of v0, /device:TPU:1, one launch (start us, length us, event | category | flops | bytes accessed | tf_op | source)
XLA Modules:
  0.0 1086.3 jit_solution(5104642623732953517)
XLA Ops:
  7.2 0.0 copy-start
  7.2 0.0 all-gather.2.cloned.1.call-start
  7.2 1.0 fusion.118
  8.2 4.9 collective-permute-start.1
  13.2 1.9 collective-permute-start
  15.2 2.6 constant_dynamic-update-slice_fusion.1
  17.8 1.0 collective-permute-done
  18.8 1.4 collective-permute-start.2
  20.3 4.0 collective-permute-start.3
  24.3 1.0 collective-permute-done.3
  25.3 12.3 %divide_add_fusion.1 = f32[64,128,128]{2,1,0:T(8,128)S(1)} fusion(f32[64,128,128]{2,1,0:T(8,128)S(1)} %copy-done.1, f32[66,128,128]{2,1,0:T(8,128)S(1)} %constant_dynamic-update-slice_fusion, f32[66,1,128]{2,1,0:T(1,128)S(1)} %collective-permute-done.3, f32[66,1,128]{2,1,0:T(1,128)S(1)} %collective-permute-done.2, ...), kind=kLoop, calls=%fused_computation.77 | loop fusion | flops 63963136 | bytes 17106944 | tf_op jit(solution)/shard_map/add | solution.py:40
  37.6 1.9 collective-permute-start.4
  39.5 3.9 collective-permute-start.5
  43.5 0.0 collective-permute-done.4
  43.5 1.3 collective-permute-done.5
  44.8 1.3 collective-permute-start.6
  46.2 4.6 collective-permute-start.7
  50.7 1.0 collective-permute-done.7
  51.7 14.4 %divide_add_fusion = f32[64,128,128]{2,1,0:T(8,128)S(1)} fusion(f32[64,128,128]{2,1,0:T(8,128)S(1)} %divide_add_fusion.1, f32[1,128,128]{2,1,0:T(8,128)S(1)} %collective-permute-done.4, f32[1,128,128]{2,1,0:T(8,128)S(1)} %collective-permute-done.5, f32[66,1,128]{2,1,0:T(1,128)S(1)} %collective-permute-done.7, f32[66,1,128]{2,1,0:T(1,128)S(1)} %collective-permute-done.6, ...), kind=kLoop, calls=%fused_computation.76 | loop fusion | flops 68157440 | bytes 12781568 | tf_op jit(solution)/shard_map/add | solution.py:40
  66.1 0.0 copy-start.3
  66.2 2.0 copy-done.3
  68.2 3.6 convolution_bitcast_fusion
  71.8 0.0 copy-start.8
  71.8 2.6 copy.106
  74.5 0.0 all-gather.2.cloned.1.call-update
  74.6 5.1 collective-permute-start.8
  79.7 2.1 collective-permute-start.9
  81.8 0.1 multiply_reduce_fusion.3
  81.9 0.7 fusion.58
  82.7 1.8 collective-permute-done.9
  84.6 1.9 fusion.50
  86.4 3.3 fusion.52
  89.8 904.3 %all-gather.2.cloned.1.call-done = f32[3,262144]{0,1:T(8,128)} async-done(((f32[3,8192]{0,1:T(8,128)}), f32[3,262144]{0,1:T(8,128)}) %all-gather.2.cloned.1.call-update) | async-done | bytes 3145744 | tf_op jit(solution)/shard_map/all_gather | solution.py:82
  994.1 59.9 %gather_fusion = f32[4096,3]{1,0:T(8,128)} fusion(f32[3,262144]{0,1:T(8,128)} %all-gather.2.cloned.1.call-done, s32[4096]{0:T(1024)S(1)} %broadcast_clamp_fusion), kind=kCustom, calls=%fused_computation | custom fusion | bytes 114688 | tf_op jit(solution)/shard_map/jit(_take)/gather | solution.py:83
  1054.0 2.2 copy.107
  1056.2 5.0 multiply_reduce_fusion.2
  1061.2 0.1 fusion.103
  1061.3 0.1 fusion.100
  1061.4 0.2 multiply_reduce_fusion.1
  1061.6 3.3 collective-permute-start.10
  1064.8 2.1 collective-permute-start.11
  1067.0 2.7 collective-permute-done.11
  1069.7 3.3 fusion.48
  1073.1 1.9 fusion.46
  1075.0 3.4 multiply_reduce_fusion
  1078.4 0.1 subtract_bitcast_fusion.2
  1078.4 0.1 subtract_bitcast_fusion.1
  1078.6 0.9 multiply_add_fusion
  (38 shorter events, 0.4 us)
Async XLA Ops:
  7.2 77.4 %copy-start = (f32[1,32,128,128]{3,2,1,0:T(8,128)S(1)}, f32[1,32,128,128]{3,2,1,0:T(8,128)}, u32[]{:S(2)}) copy-start(f32[1,32,128,128]{3,2,1,0:T(8,128)} %param.17) | copy-start | bytes 6291460
  7.2 986.9 %all-gather.2.cloned.1.call-start = ((), (), s32[]{:S(2)}) async-start(), calls=%async_computation | async-start | bytes 138412032 | tf_op jit(solution)/shard_map/all_gather | solution.py:82
  8.2 6.9 collective-permute-start.1
  13.2 5.6 collective-permute-start
  15.1 10.1 copy-start.1
  15.2 10.1 copy-start.2
  18.8 5.4 collective-permute-start.2
  20.3 5.0 collective-permute-start.3
  37.6 5.9 collective-permute-start.4
  39.5 5.3 collective-permute-start.5
  44.8 5.9 collective-permute-start.6
  46.1 22.0 %copy-start.7 = (f32[3,128]{1,0:T(4,128)S(1)}, f32[3,128]{1,0:T(4,128)}, u32[]{:S(2)}) copy-start(f32[3,128]{1,0:T(4,128)} %param.11) | copy-start | bytes 4612
  46.2 5.6 collective-permute-start.7
  66.1 2.0 copy-start.3
  71.8 2.7 copy-start.5
  71.8 10.1 copy-start.6
  71.8 10.1 copy-start.8
  71.8 10.1 copy-start.9
  74.6 8.2 collective-permute-start.8
  79.7 4.9 collective-permute-start.9
  1061.2 13.8 %copy-start.4 = (f32[1,32,128,128]{3,2,1,0:T(8,128)S(1)}, f32[1,32,128,128]{3,2,1,0:T(8,128)}, u32[]{:S(2)}) copy-start(f32[1,32,128,128]{3,2,1,0:T(8,128)} %param.16) | copy-start | bytes 6291460
  1061.6 5.4 collective-permute-start.10
  1064.8 4.9 collective-permute-start.11
Sparse Core Ops, SparseCore 0:
  74.6 919.3 all-gather.1
where the time goes:
time: 1090 us
  waiting for transfers between devices  913 us (84%)
  local copies, waits for them, and re-layouts  70.6 us (6%)
  starting transfers between devices  36.7 us (3%)
  other arithmetic  28.2 us (3%)
  matrix products  23.2 us (2%)
  between operations  14.5 us (1%)
    all_gather x1, waiting for transfers between devices, per_device(): table = lax.all_gather(surface, 'track', axis=1, tiled=True)  904 us
    gather x2, local copies, waits for them, and re-layouts, per_device(): applied = jnp.take(table, cells, axis=1)  62.1 us
    add x2, other arithmetic, relax_sweep(): return center + 0.8 * numer / denom  26.7 us
    ppermute x6, starting transfers between devices, extended(): lax.ppermute(lax.slice_in_dim(block, block.shape[dim] - width, None, axis...  25.8 us
  transfers between devices with their start and end apart: 13, of which 7 were waited for; matrix products, arithmetic and copies ran while one was open for 1% of the time, Pallas kernels for 0%

commit v1 on v0

--- a/solution.py
+++ b/solution.py
@@ -79,7 +79,9 @@
         3, rows_x * rows_y
     )
     cells = footprint[0]
-    table = lax.all_gather(surface, "track", axis=1, tiled=True)
+    table = jnp.concatenate(
+        lax.all_to_all(jnp.stack([surface] * lax.axis_size("track")), "track", 0, 0), axis=1
+    )
     applied = jnp.take(table, cells, axis=1)
     n_prof = temp_profile.shape[0]
     onehot = (temp_index[0][None, :] == jnp.arange(n_prof, dtype=jnp.int32)[:, None]).astype(

time: 1090 us -> 299 us (0.27)
  the two profiles are of different devices: /device:TPU:1 before, /device:TPU:5 now
where the time goes in v1:
time: 299 us; the launch traced here: 298 us
  local copies, waits for them, and re-layouts  130 us (43%)
  waiting for transfers between devices  61.3 us (21%)
  starting transfers between devices  54.4 us (18%)
  other arithmetic  28.3 us (9%)
  matrix products  23.2 us (8%)
    gather x2, local copies, waits for them, and re-layouts, per_device(): applied = jnp.take(table, cells, axis=1)  61.7 us
    reshape x1, local copies, waits for them, and re-layouts, per_device(): jnp.concatenate(lax.all_to_all(jnp.stack([surface] * lax.axis_size('track...  59.3 us
    all_to_all x1, waiting for transfers between devices, per_device(): lax.all_to_all(jnp.stack([surface] * lax.axis_size('track')), 'track', 0, 0)  29.9 us
    add x2, other arithmetic, relax_sweep(): return center + 0.8 * numer / denom  26.7 us
    ppermute x6, starting transfers between devices, extended(): lax.ppermute(lax.slice_in_dim(block, block.shape[dim] - width, None, axis...  24.9 us
    ppermute x6, waiting for transfers between devices, extended(): lax.ppermute(lax.slice_in_dim(block, 0, width, axis=dim), axis, backward)  19.1 us
    all_to_all x1, starting transfers between devices, per_device(): lax.all_to_all(jnp.stack([surface] * lax.axis_size('track')), 'track', 0, 0)  16.5 us
    ppermute x6, starting transfers between devices, extended(): lax.ppermute(lax.slice_in_dim(block, 0, width, axis=dim), axis, backward)  13 us
  transfers between devices with their start and end apart: 13, of which 8 were waited for; matrix products, arithmetic and copies ran while one was open for 3% of the time, Pallas kernels for 0%

profile of v1, /device:TPU:5, one launch (start us, length us, event | category | flops | bytes accessed | tf_op | source)
XLA Modules:
  0.0 297.8 jit_solution(9152217867691268218)
XLA Ops:
  0.6 0.0 copy-start
  0.6 1.0 fusion.118
  1.7 4.1 %collective-permute-start.1 = (f32[1,128,128]{2,1,0:T(8,128)S(1)}, f32[1,128,128]{2,1,0:T(8,128)S(1)}, u32[]{:S(2)}, u32[]{:S(2)}) collective-permute-start(f32[1,128,128]{2,1,0:T(8,128)S(1)} %get-tuple-element.21), channel_id=1, source_target_pairs={{0,32},{32,64},{64,96},{1,33},{33,65},{65,97},{2,34},{34,66},{66,9... | collective-permute-start | bytes 196616 | tf_op jit(solution)/shard_map/ppermute | solution.py:14
  5.8 1.9 collective-permute-start
  7.8 2.6 constant_dynamic-update-slice_fusion.1
  10.4 1.0 collective-permute-done
  11.4 2.3 collective-permute-start.2
  13.7 3.1 %collective-permute-start.3 = (f32[66,1,128]{2,1,0:T(1,128)S(1)}, f32[66,1,128]{2,1,0:T(1,128)S(1)}, u32[]{:S(2)}, u32[]{:S(2)}) collective-permute-start(f32[66,1,128]{2,1,0:T(1,128)S(1)} %get-tuple-element.17), channel_id=1, source_target_pairs={{0,1},{1,2},{2,3},{3,4},{4,5},{5,6},{6,7},{7,8},{8,9},{9,10},{10,1... | collective-permute-start | bytes 101384 | tf_op jit(solution)/shard_map/ppermute | solution.py:14
  16.9 1.5 collective-permute-done.3
  18.4 12.3 %divide_add_fusion.1 = f32[64,128,128]{2,1,0:T(8,128)S(1)} fusion(f32[64,128,128]{2,1,0:T(8,128)S(1)} %copy-done.1, f32[66,128,128]{2,1,0:T(8,128)S(1)} %constant_dynamic-update-slice_fusion, f32[66,1,128]{2,1,0:T(1,128)S(1)} %collective-permute-done.3, f32[66,1,128]{2,1,0:T(1,128)S(1)} %collective-permute-done.2, ...), kind=kLoop, calls=%fused_computation.77 | loop fusion | flops 63963136 | bytes 17106944 | tf_op jit(solution)/shard_map/add | solution.py:40
  30.7 1.9 collective-permute-start.4
  32.7 4.2 %collective-permute-start.5 = (f32[1,128,128]{2,1,0:T(8,128)S(1)}, f32[1,128,128]{2,1,0:T(8,128)S(1)}, u32[]{:S(2)}, u32[]{:S(2)}) collective-permute-start(f32[1,128,128]{2,1,0:T(8,128)S(1)} %get-tuple-element.18), channel_id=1, source_target_pairs={{0,32},{32,64},{64,96},{1,33},{33,65},{65,97},{2,34},{34,66},{66,9... | collective-permute-start | bytes 196616 | tf_op jit(solution)/shard_map/ppermute | solution.py:14
  36.9 0.0 collective-permute-done.4
  36.9 1.3 collective-permute-done.5
  38.3 2.2 collective-permute-start.6
  40.4 5.4 %collective-permute-start.7 = (f32[66,1,128]{2,1,0:T(1,128)S(1)}, f32[66,1,128]{2,1,0:T(1,128)S(1)}, u32[]{:S(2)}, u32[]{:S(2)}) collective-permute-start(f32[66,1,128]{2,1,0:T(1,128)S(1)} %get-tuple-element.15), channel_id=1, source_target_pairs={{0,1},{1,2},{2,3},{3,4},{4,5},{5,6},{6,7},{7,8},{8,9},{9,10},{10,1... | collective-permute-start | bytes 101384 | tf_op jit(solution)/shard_map/ppermute | solution.py:14
  45.8 1.0 collective-permute-done.7
  46.8 14.4 %divide_add_fusion = f32[64,128,128]{2,1,0:T(8,128)S(1)} fusion(f32[64,128,128]{2,1,0:T(8,128)S(1)} %divide_add_fusion.1, f32[1,128,128]{2,1,0:T(8,128)S(1)} %collective-permute-done.4, f32[1,128,128]{2,1,0:T(8,128)S(1)} %collective-permute-done.5, f32[66,1,128]{2,1,0:T(1,128)S(1)} %collective-permute-done.7, f32[66,1,128]{2,1,0:T(1,128)S(1)} %collective-permute-done.6, ...), kind=kLoop, calls=%fused_computation.76 | loop fusion | flops 68157440 | bytes 12781568 | tf_op jit(solution)/shard_map/add | solution.py:40
  61.2 0.0 copy-start.3
  61.3 2.0 copy-done.3
  63.3 3.6 %convolution_bitcast_fusion = f32[3,8192]{1,0:T(4,128)S(1)} fusion(f32[64,128,128]{2,1,0:T(8,128)S(1)} %divide_add_fusion, f32[3,128]{1,0:T(4,128)S(1)} %copy-done.7), kind=kOutput, calls=%fused_computation.5 | convolution fusion | flops 37748736 | bytes 4294144 | tf_op jit(solution)/shard_map/kz,xyz->kxy/dot_general | solution.py:78
  66.9 2.9 stack.55
  69.8 16.5 %all-to-all-start = ((f32[32,3,8192]{2,1,0:T(4,128)}), f32[32,3,8192]{2,1,0:T(4,128)}, u32[]{:S(2)}, u32[]{:S(2)}) async-start(f32[32,3,8192]{2,1,0:T(4,128)} %stack.55), calls=%async_computation | async-start | bytes 8388608 | tf_op jit(solution)/shard_map/all_to_all | solution.py:83
  86.4 6.0 %collective-permute-start.8 = (f32[3,128]{1,0:T(4,128)S(1)}, f32[3,128]{1,0:T(4,128)S(1)}, u32[]{:S(2)}, u32[]{:S(2)}) collective-permute-start(f32[3,128]{1,0:T(4,128)S(1)} %get-tuple-element.24), channel_id=1, source_target_pairs={{0,32},{32,64},{64,96},{1,33},{33,65},{65,97},{2,34},{34,66},{66,9... | collective-permute-start | bytes 4616 | tf_op jit(solution)/shard_map/ppermute | solution.py:14
  92.3 2.1 collective-permute-start.9
  94.5 0.1 multiply_reduce_fusion.3
  94.6 0.7 fusion.58
  95.4 8.4 %collective-permute-done.8 = f32[3,128]{1,0:T(4,128)S(1)} collective-permute-done((f32[3,128]{1,0:T(4,128)S(1)}, f32[3,128]{1,0:T(4,128)S(1)}, u32[]{:S(2)}, u32[]{:S(2)}) %collective-permute-start.8) | collective-permute-done | bytes 1568 | tf_op jit(solution)/shard_map/ppermute | solution.py:14
  103.8 15.9 %collective-permute-done.9 = f32[3,128]{1,0:T(4,128)S(1)} collective-permute-done((f32[3,128]{1,0:T(4,128)S(1)}, f32[3,128]{1,0:T(4,128)S(1)}, u32[]{:S(2)}, u32[]{:S(2)}) %collective-permute-start.9) | collective-permute-done | bytes 1568 | tf_op jit(solution)/shard_map/ppermute | solution.py:17
  119.7 1.9 fusion.50
  121.5 3.3 %fusion.52 = f32[32,3,128]{2,1,0:T(4,128)S(1)} fusion(f32[1,32,128,128]{3,2,1,0:T(8,128)S(1)} %copy-done, f32[3,128]{1,0:T(4,128)S(1)} %collective-permute-done.9, f32[3,4096]{1,0:T(4,128)S(1)} %bitcast.166, f32[3,128]{1,0:T(4,128)S(1)} %collective-permute-done.8), kind=kOutput, calls=%fused_computation.84 | convolution fusion | flops 18900480 | bytes 2198528 | tf_op jit(solution)/shard_map/kij,ckj->cki/dot_general | solution.py:100
  124.9 29.9 %all-to-all-done = f32[32,3,8192]{2,1,0:T(4,128)} async-done(((f32[32,3,8192]{2,1,0:T(4,128)}), f32[32,3,8192]{2,1,0:T(4,128)}, u32[]{:S(2)}, u32[]{:S(2)}) %all-to-all-start) | async-done | bytes 3145760 | tf_op jit(solution)/shard_map/all_to_all | solution.py:83
  154.8 59.3 %copy.106 = f32[3,32,8192]{0,2,1:T(8,128)} copy(f32[3,32,8192]{2,0,1:T(4,128)} %bitcast.5) | data formatting | bytes 6291456 | tf_op jit(solution)/shard_map/reshape | solution.py:82
  214.1 59.5 %gather_fusion = f32[4096,3]{1,0:T(8,128)} fusion(f32[3,262144]{0,1:T(8,128)} %bitcast.6, s32[4096]{0:T(1024)S(1)} %broadcast_clamp_fusion), kind=kCustom, calls=%fused_computation | custom fusion | bytes 114688 | tf_op jit(solution)/shard_map/jit(_take)/gather | solution.py:85
  273.6 2.2 copy.107
  275.8 5.0 %multiply_reduce_fusion.2 = (f32[4096]{0:T(1024)S(1)}, f32[3,4096]{1,0:T(4,128)S(1)}) fusion(f32[3,1,4096]{2,1,0:T(1,128)S(1)} %copy-done.5, f32[3,4096]{1,0:T(4,128)S(1)} %bitcast.167, f32[4096]{0:T(1024)S(1)} %subtract_multiply_fusion.1, f32[32,3,128]{2,1,0:T(4,128)S(1)} %fusion.50, f32[32,3,128]{2,1,0:T(4,128)S(1)} %fusion.52, ...), kind=kOutput, calls=%fused_computation.115 | convolution fusion | flops 18994688 | bytes 2432000 | tf_op jit(solution)/shard_map/kij,ckj->cki/dot_general | solution.py:99
  280.8 0.1 fusion.103
  280.9 0.1 fusion.100
  281.0 0.2 multiply_reduce_fusion.1
  281.2 2.1 collective-permute-start.10
  283.2 2.6 collective-permute-start.11
  285.9 2.2 collective-permute-done.11
  288.1 3.3 %fusion.48 = f32[32,3,128]{2,1,0:T(4,128)S(1)} fusion(f32[1,32,128,128]{3,2,1,0:T(8,128)S(1)} %copy-done, f32[3,128]{1,0:T(4,128)S(1)} %collective-permute-done.11, f32[3,4096]{1,0:T(4,128)S(1)} %get-tuple-element.8, f32[3,128]{1,0:T(4,128)S(1)} %collective-permute-done.10), kind=kOutput, calls=%fused_computation.80 | convolution fusion | flops 18900480 | bytes 2198528 | tf_op jit(solution)/shard_map/kij,ckj->cki/dot_general | solution.py:100
  291.5 1.9 fusion.46
  293.3 3.4 %multiply_reduce_fusion = (f32[4096]{0:T(1024)S(1)}, f32[3,4096]{1,0:T(4,128)S(1)}) fusion(f32[3,4096]{1,0:T(4,128)S(1)} %get-tuple-element.8, f32[4096]{0:T(1024)S(1)} %subtract_multiply_fusion, f32[32,3,128]{2,1,0:T(4,128)S(1)} %fusion.46, f32[32,3,128]{2,1,0:T(4,128)S(1)} %fusion.48, f32[1,32,128,128]{3,2,1,0:T(8,128)S(1)} %copy-done.4, ...), kind=kOutput, calls=%fused_computation.113 | convolution fusion | flops 18994688 | bytes 2382848 | tf_op jit(solution)/shard_map/kij,ckj->cki/dot_general | solution.py:99
  296.7 0.1 subtract_bitcast_fusion.2
  296.8 0.1 subtract_bitcast_fusion.1
  297.0 0.9 multiply_add_fusion
  (38 shorter events, 0.4 us)
Async XLA Ops:
  0.6 119.0 %copy-start = (f32[1,32,128,128]{3,2,1,0:T(8,128)S(1)}, f32[1,32,128,128]{3,2,1,0:T(8,128)}, u32[]{:S(2)}) copy-start(f32[1,32,128,128]{3,2,1,0:T(8,128)} %param.17) | copy-start | bytes 6291460
  1.7 6.0 %collective-permute-start.1 = (f32[1,128,128]{2,1,0:T(8,128)S(1)}, f32[1,128,128]{2,1,0:T(8,128)S(1)}, u32[]{:S(2)}, u32[]{:S(2)}) collective-permute-start(f32[1,128,128]{2,1,0:T(8,128)S(1)} %get-tuple-element.21), channel_id=1, source_target_pairs={{0,32},{32,64},{64,96},{1,33},{33,65},{65,97},{2,34},{34,66},{66,9... | collective-permute-start | bytes 196616 | tf_op jit(solution)/shard_map/ppermute | solution.py:14
  5.8 5.6 %collective-permute-start = (f32[1,128,128]{2,1,0:T(8,128)S(1)}, f32[1,128,128]{2,1,0:T(8,128)S(1)}, u32[]{:S(2)}, u32[]{:S(2)}) collective-permute-start(f32[1,128,128]{2,1,0:T(8,128)S(1)} %get-tuple-element.20), channel_id=1, source_target_pairs={{32,0},{64,32},{96,64},{33,1},{65,33},{97,65},{34,2},{66,34},{98,6... | collective-permute-start | bytes 196616 | tf_op jit(solution)/shard_map/ppermute | solution.py:17
  7.7 10.7 %copy-start.1 = (f32[64,128,128]{2,1,0:T(8,128)S(1)}, f32[64,128,128]{2,1,0:T(8,128)}, u32[]{:S(2)}) copy-start(f32[64,128,128]{2,1,0:T(8,128)} %param.9) | copy-start | bytes 12582916
  7.8 10.7 %copy-start.2 = (f32[64,128,128]{2,1,0:T(8,128)S(1)}, f32[64,128,128]{2,1,0:T(8,128)}, u32[]{:S(2)}) copy-start(f32[64,128,128]{2,1,0:T(8,128)} %param.10) | copy-start | bytes 12582916
  11.4 5.4 %collective-permute-start.2 = (f32[66,1,128]{2,1,0:T(1,128)S(1)}, f32[66,1,128]{2,1,0:T(1,128)S(1)}, u32[]{:S(2)}, u32[]{:S(2)}) collective-permute-start(f32[66,1,128]{2,1,0:T(1,128)S(1)} %get-tuple-element.16), channel_id=1, source_target_pairs={{1,0},{2,1},{3,2},{4,3},{5,4},{6,5},{7,6},{8,7},{9,8},{10,9},{11,1... | collective-permute-start | bytes 101384 | tf_op jit(solution)/shard_map/ppermute | solution.py:17
  13.7 4.7 %collective-permute-start.3 = (f32[66,1,128]{2,1,0:T(1,128)S(1)}, f32[66,1,128]{2,1,0:T(1,128)S(1)}, u32[]{:S(2)}, u32[]{:S(2)}) collective-permute-start(f32[66,1,128]{2,1,0:T(1,128)S(1)} %get-tuple-element.17), channel_id=1, source_target_pairs={{0,1},{1,2},{2,3},{3,4},{4,5},{5,6},{6,7},{7,8},{8,9},{9,10},{10,1... | collective-permute-start | bytes 101384 | tf_op jit(solution)/shard_map/ppermute | solution.py:14
  30.7 6.2 %collective-permute-start.4 = (f32[1,128,128]{2,1,0:T(8,128)S(1)}, f32[1,128,128]{2,1,0:T(8,128)S(1)}, u32[]{:S(2)}, u32[]{:S(2)}) collective-permute-start(f32[1,128,128]{2,1,0:T(8,128)S(1)} %get-tuple-element.19), channel_id=1, source_target_pairs={{32,0},{64,32},{96,64},{33,1},{65,33},{97,65},{34,2},{66,34},{98,6... | collective-permute-start | bytes 196616 | tf_op jit(solution)/shard_map/ppermute | solution.py:17
  32.7 5.6 %collective-permute-start.5 = (f32[1,128,128]{2,1,0:T(8,128)S(1)}, f32[1,128,128]{2,1,0:T(8,128)S(1)}, u32[]{:S(2)}, u32[]{:S(2)}) collective-permute-start(f32[1,128,128]{2,1,0:T(8,128)S(1)} %get-tuple-element.18), channel_id=1, source_target_pairs={{0,32},{32,64},{64,96},{1,33},{33,65},{65,97},{2,34},{34,66},{66,9... | collective-permute-start | bytes 196616 | tf_op jit(solution)/shard_map/ppermute | solution.py:14
  38.3 7.6 %collective-permute-start.6 = (f32[66,1,128]{2,1,0:T(1,128)S(1)}, f32[66,1,128]{2,1,0:T(1,128)S(1)}, u32[]{:S(2)}, u32[]{:S(2)}) collective-permute-start(f32[66,1,128]{2,1,0:T(1,128)S(1)} %get-tuple-element.14), channel_id=1, source_target_pairs={{1,0},{2,1},{3,2},{4,3},{5,4},{6,5},{7,6},{8,7},{9,8},{10,9},{11,1... | collective-permute-start | bytes 101384 | tf_op jit(solution)/shard_map/ppermute | solution.py:17
  40.4 22.8 %copy-start.7 = (f32[3,128]{1,0:T(4,128)S(1)}, f32[3,128]{1,0:T(4,128)}, u32[]{:S(2)}) copy-start(f32[3,128]{1,0:T(4,128)} %param.11) | copy-start | bytes 4612
  40.4 6.4 %collective-permute-start.7 = (f32[66,1,128]{2,1,0:T(1,128)S(1)}, f32[66,1,128]{2,1,0:T(1,128)S(1)}, u32[]{:S(2)}, u32[]{:S(2)}) collective-permute-start(f32[66,1,128]{2,1,0:T(1,128)S(1)} %get-tuple-element.15), channel_id=1, source_target_pairs={{0,1},{1,2},{2,3},{3,4},{4,5},{5,6},{6,7},{7,8},{8,9},{9,10},{10,1... | collective-permute-start | bytes 101384 | tf_op jit(solution)/shard_map/ppermute | solution.py:14
  61.2 2.0 copy-start.3
  69.8 16.5 %copy-start.5 = (f32[3,1,4096]{2,1,0:T(1,128)S(1)}, f32[3,1,4096]{2,1,0:T(1,128)}, u32[]{:S(2)}) copy-start(f32[3,1,4096]{2,1,0:T(1,128)} %param.12) | copy-start | bytes 147460
  69.8 24.7 %copy-start.6 = (s32[1,4096]{1,0:T(1,128)S(1)}, s32[1,4096]{1,0:T(1,128)}, u32[]{:S(2)}) copy-start(s32[1,4096]{1,0:T(1,128)} %param.13) | copy-start | bytes 49156
  69.8 24.8 %copy-start.8 = (s32[1,4096]{1,0:T(1,128)S(1)}, s32[1,4096]{1,0:T(1,128)}, u32[]{:S(2)}) copy-start(s32[1,4096]{1,0:T(1,128)} %param.14) | copy-start | bytes 49156
  69.8 24.8 %copy-start.9 = (f32[128]{0:T(128)S(1)}, f32[128]{0:T(128)}, u32[]{:S(2)}) copy-start(f32[128]{0:T(128)} %param.15) | copy-start | bytes 1540
  69.8 85.0 %all-to-all-start = ((f32[32,3,8192]{2,1,0:T(4,128)}), f32[32,3,8192]{2,1,0:T(4,128)}, u32[]{:S(2)}, u32[]{:S(2)}) async-start(f32[32,3,8192]{2,1,0:T(4,128)} %stack.55), calls=%async_computation | async-start | bytes 8388608 | tf_op jit(solution)/shard_map/all_to_all | solution.py:83
  86.4 17.4 %collective-permute-start.8 = (f32[3,128]{1,0:T(4,128)S(1)}, f32[3,128]{1,0:T(4,128)S(1)}, u32[]{:S(2)}, u32[]{:S(2)}) collective-permute-start(f32[3,128]{1,0:T(4,128)S(1)} %get-tuple-element.24), channel_id=1, source_target_pairs={{0,32},{32,64},{64,96},{1,33},{33,65},{65,97},{2,34},{34,66},{66,9... | collective-permute-start | bytes 4616 | tf_op jit(solution)/shard_map/ppermute | solution.py:14
  92.3 27.3 %collective-permute-start.9 = (f32[3,128]{1,0:T(4,128)S(1)}, f32[3,128]{1,0:T(4,128)S(1)}, u32[]{:S(2)}, u32[]{:S(2)}) collective-permute-start(f32[3,128]{1,0:T(4,128)S(1)} %get-tuple-element.25), channel_id=1, source_target_pairs={{32,0},{64,32},{96,64},{33,1},{65,33},{97,65},{34,2},{66,34},{98,6... | collective-permute-start | bytes 4616 | tf_op jit(solution)/shard_map/ppermute | solution.py:17
  280.8 12.6 %copy-start.4 = (f32[1,32,128,128]{3,2,1,0:T(8,128)S(1)}, f32[1,32,128,128]{3,2,1,0:T(8,128)}, u32[]{:S(2)}) copy-start(f32[1,32,128,128]{3,2,1,0:T(8,128)} %param.16) | copy-start | bytes 6291460
  281.2 4.7 %collective-permute-start.10 = (f32[3,128]{1,0:T(4,128)S(1)}, f32[3,128]{1,0:T(4,128)S(1)}, u32[]{:S(2)}, u32[]{:S(2)}) collective-permute-start(f32[3,128]{1,0:T(4,128)S(1)} %get-tuple-element.22), channel_id=1, source_target_pairs={{0,32},{32,64},{64,96},{1,33},{33,65},{65,97},{2,34},{34,66},{66,9... | collective-permute-start | bytes 4616 | tf_op jit(solution)/shard_map/ppermute | solution.py:14
  283.2 4.9 %collective-permute-start.11 = (f32[3,128]{1,0:T(4,128)S(1)}, f32[3,128]{1,0:T(4,128)S(1)}, u32[]{:S(2)}, u32[]{:S(2)}) collective-permute-start(f32[3,128]{1,0:T(4,128)S(1)} %get-tuple-element.23), channel_id=1, source_target_pairs={{32,0},{64,32},{96,64},{33,1},{65,33},{97,65},{34,2},{66,34},{98,6... | collective-permute-start | bytes 4616 | tf_op jit(solution)/shard_map/ppermute | solution.py:17
